TPU v7x, 32 devices: a whole 2x2x4 slice. The times are simulated.
32 devices in a mesh: fsdp: 4 (over y, x), ctx: 4 (over z), tp: 2 (over core).
Axes of the slice: x: 2, y: 2, z: 4, core: 2. Of those that a mesh axis runs over, the one named last changes fastest.
Arguments:
- tokens: bfloat16 [8, 2048, 896], P('fsdp', 'ctx'), may hold values from -6 to 6
- cotangent: bfloat16 [8, 2048, 896], P('fsdp', 'ctx'), may hold values from -6 to 6
- segments: int32 [8, 2048], P('fsdp'), may hold values from 0 to 3, as said below
- positions: int32 [8, 2048], P('fsdp', 'ctx'), may hold values from 0 to 2044, as said below
- norm_one: bfloat16 [896], replicated, may hold values from 0.5 to 1.5
- qkv_weight: bfloat16 [896, 2, 576], P(('fsdp', 'ctx'), 'tp'), may hold values from -0.1875 to 0.1875
- qkv_bias: bfloat16 [2, 576], P('tp'), may hold values from -3 to 3
- out_weight: bfloat16 [896, 896], P(('fsdp', 'ctx'), 'tp'), may hold values from -0.75 to 0.75
- norm_two: bfloat16 [896], replicated, may hold values from 0.5 to 1.5
- gate_weight: bfloat16 [896, 4864], P(('fsdp', 'ctx'), 'tp'), may hold values from -0.1875 to 0.1875
- up_weight: bfloat16 [896, 4864], P(('fsdp', 'ctx'), 'tp'), may hold values from -0.1875 to 0.1875
- down_weight: bfloat16 [896, 4864], P(('fsdp', 'ctx'), 'tp'), may hold values from -0.078125 to 0.078125
Outputs:
- block_out: bfloat16 [8, 2048, 896], P('fsdp', ('ctx', 'tp'))
- input_grad: float32 [8, 2048, 896], P('fsdp', 'ctx')
- norm_one_grad: float32 [896], replicated
- qkv_weight_grad: float32 [896, 2, 576], P(('fsdp', 'ctx'), 'tp')
- qkv_bias_grad: float32 [2, 576], P('tp')
- out_weight_grad: float32 [896, 896], P(('fsdp', 'ctx'), 'tp')
- norm_two_grad: float32 [896], replicated
- gate_weight_grad: float32 [896, 4864], P(('fsdp', 'ctx'), 'tp')
- up_weight_grad: float32 [896, 4864], P(('fsdp', 'ctx'), 'tp')
- down_weight_grad: float32 [896, 4864], P(('fsdp', 'ctx'), 'tp')
Inputs may be any that keep to these rules, and one draw needn't show every extreme that they name: `segments`: each sequence holds exactly 4 documents, numbered from 0 in order, each a contiguous run; the first token is document 0. `positions`: each token's offset from the first token of its document; the largest is reached in every draw.
All inputs are finite; a program needn't handle non-finite values.
Results may differ from a plain program's by a relative error of at most 0.02.
Values may be sent and summed in bfloat16 or wider, within the bound.
No kernel may reach another device: no remote copies, remote signals or barrier semaphores. Data moves between devices by JAX's collectives and lax.ppermute only.
A program may use at most 256 MiB of HBM per device.

v0:
```python
import jax
import jax.numpy as jnp
from jax import lax
from jax.sharding import PartitionSpec as P

HD = 64
GROUP = 7
epsilon = 1e-06
rope_base = 1000000.0
masked_value = -1e30
contract_rows = (((0,), (0,)), ((), ()))
contract_last = (((1,), (1,)), ((), ()))


def rotary_tables(positions):
    half_dim = HD // 2
    frequency = rope_base ** (-(jnp.arange(half_dim, dtype=jnp.float32) * 2.0) / HD)
    angles = positions.astype(jnp.float32)[..., None] * frequency
    cosine = jnp.cos(angles)
    sine_table = jnp.sin(angles)
    return (jnp.concatenate([cosine, cosine], -1), jnp.concatenate([sine_table, sine_table], -1))


def rotate(values, cosine, sine_table):
    half_dim = values.shape[-1] // 2
    turned = jnp.concatenate([-values[..., half_dim:], values[..., :half_dim]], -1)
    return values * cosine + turned * sine_table


def masked_scores(query_one, key_one, own_segment, all_segments, first_row):
    raw_scores = jnp.einsum(
        "qhgd,khd->hgqk", query_one, key_one, preferred_element_type=jnp.float32
    ) * HD ** (-0.5)
    query_index = first_row + jnp.arange(own_segment.shape[0], dtype=jnp.int32)
    key_index = jnp.arange(all_segments.shape[0], dtype=jnp.int32)
    allowed = (own_segment[:, None] == all_segments[None, :]) & (
        key_index[None, :] <= query_index[:, None]
    )
    return jnp.where(allowed, raw_scores, masked_value)


def shards(
    tokens,
    cotangent,
    segments,
    positions,
    norm_one,
    qkv_weight,
    qkv_bias,
    out_weight,
    norm_two,
    gate_weight,
    up_weight,
    down_weight,
):
    seq_count, block_len, model_width = tokens.shape
    row_count = seq_count * block_len
    kv_local = qkv_weight.shape[1]
    per_group = qkv_weight.shape[2]
    q_width = out_weight.shape[1]
    first_row = lax.axis_index("ctx") * block_len
    half_len = block_len // lax.axis_size("tp")
    half_start = lax.axis_index("tp") * half_len

    def own_rows(values):
        return lax.dynamic_slice_in_dim(values, half_start, half_len, 1)

    attention_full = (
        lax.all_gather(qkv_weight, ("fsdp", "ctx"), axis=0, tiled=True),
        lax.all_gather(out_weight, ("fsdp", "ctx"), axis=0, tiled=True),
    )
    qkv_full = attention_full[0].reshape(model_width, kv_local * per_group)
    out_full = attention_full[1]
    inputs_block = tokens.astype(jnp.float32)
    inputs = inputs_block.reshape(row_count, model_width)
    gain_one = norm_one.astype(jnp.float32)
    scale_one = lax.rsqrt(jnp.mean(inputs * inputs, -1, keepdims=True) + epsilon)
    unit_one = inputs * scale_one
    normed = (unit_one * gain_one).astype(jnp.bfloat16)
    projected = jnp.dot(normed, qkv_full, preferred_element_type=jnp.float32) + qkv_bias.astype(
        jnp.float32
    )
    grouped = projected.reshape(seq_count, block_len, kv_local, GROUP + 2, HD)
    cosine, sine_table = rotary_tables(positions)
    queries = rotate(
        grouped[:, :, :, :GROUP], cosine[:, :, None, None], sine_table[:, :, None, None]
    ).astype(jnp.bfloat16)
    key_rows = rotate(grouped[:, :, :, GROUP], cosine[:, :, None], sine_table[:, :, None]).astype(
        jnp.bfloat16
    )
    values = grouped[:, :, :, GROUP + 1].astype(jnp.bfloat16)
    kv_pack = jnp.concatenate([key_rows, values], -1)
    kv_all = lax.all_gather(kv_pack, "ctx", axis=1, tiled=True)
    own_segments = lax.dynamic_slice_in_dim(segments, first_row, block_len, 1)

    def attend(pieces):
        query_one, pack_one, own_segment, all_segments = pieces
        masked = masked_scores(query_one, pack_one[..., :HD], own_segment, all_segments, first_row)
        row_max = jnp.max(masked, -1, keepdims=True)
        exponent = jnp.exp(masked - row_max)
        row_total = jnp.sum(exponent, -1, keepdims=True)
        probability = (exponent / row_total).astype(jnp.bfloat16)
        result = jnp.einsum(
            "hgqk,khd->qhgd", probability, pack_one[..., HD:], preferred_element_type=jnp.float32
        )
        return (result, row_max + jnp.log(row_total))

    attended, log_totals = lax.map(attend, (queries, kv_all, own_segments, segments))
    mixed = attended.reshape(row_count, q_width).astype(jnp.bfloat16)
    branch_part = lax.dot_general(
        mixed, out_full, contract_last, preferred_element_type=jnp.float32
    )
    attention_sum = lax.psum_scatter(
        branch_part.reshape(seq_count, block_len, model_width).astype(jnp.bfloat16),
        "tp",
        scatter_dimension=1,
        tiled=True,
    ).astype(jnp.float32)
    middle = own_rows(inputs_block) + attention_sum
    feed_full = (
        lax.all_gather(gate_weight, ("fsdp", "ctx"), axis=0, tiled=True),
        lax.all_gather(up_weight, ("fsdp", "ctx"), axis=0, tiled=True),
        lax.all_gather(down_weight, ("fsdp", "ctx"), axis=0, tiled=True),
    )
    gate_full, up_full, down_full = feed_full
    gain_two = norm_two.astype(jnp.float32)
    scale_two = lax.rsqrt(jnp.mean(middle * middle, -1, keepdims=True) + epsilon)
    unit_two = middle * scale_two
    normed_two_half = (unit_two * gain_two).astype(jnp.bfloat16)
    normed_two = lax.all_gather(normed_two_half, "tp", axis=1, tiled=True).reshape(
        row_count, model_width
    )
    gate_act = jnp.dot(normed_two, gate_full, preferred_element_type=jnp.float32)
    up_act = jnp.dot(normed_two, up_full, preferred_element_type=jnp.float32)
    silu_gate = jax.nn.silu(gate_act)
    hidden = (silu_gate * up_act).astype(jnp.bfloat16)
    feed_part = lax.dot_general(
        hidden, down_full, contract_last, preferred_element_type=jnp.float32
    )
    feed_sum = lax.psum_scatter(
        feed_part.reshape(seq_count, block_len, model_width).astype(jnp.bfloat16),
        "tp",
        scatter_dimension=1,
        tiled=True,
    ).astype(jnp.float32)
    block_out = (middle + feed_sum).astype(jnp.bfloat16)
    attention_back = (
        lax.all_gather(qkv_weight, ("fsdp", "ctx"), axis=0, tiled=True),
        lax.all_gather(out_weight, ("fsdp", "ctx"), axis=0, tiled=True),
    )
    feed_back = (
        lax.all_gather(gate_weight, ("fsdp", "ctx"), axis=0, tiled=True),
        lax.all_gather(up_weight, ("fsdp", "ctx"), axis=0, tiled=True),
        lax.all_gather(down_weight, ("fsdp", "ctx"), axis=0, tiled=True),
    )
    qkv_back = attention_back[0].reshape(model_width, kv_local * per_group)
    out_back = attention_back[1]
    gate_back, up_back, down_back = feed_back
    upstream_low = cotangent.reshape(row_count, model_width)
    upstream_half = own_rows(cotangent).astype(jnp.float32)
    hidden_grad = jnp.dot(upstream_low, down_back, preferred_element_type=jnp.float32)
    down_weight_grad = lax.dot_general(
        upstream_low, hidden, contract_rows, preferred_element_type=jnp.float32
    )
    sigmoid = jax.nn.sigmoid(gate_act)
    gate_grad = (hidden_grad * up_act * (sigmoid * (1.0 + gate_act * (1.0 - sigmoid)))).astype(
        jnp.bfloat16
    )
    up_grad = (hidden_grad * silu_gate).astype(jnp.bfloat16)
    normed_two_part = lax.dot_general(
        gate_grad, gate_back, contract_last, preferred_element_type=jnp.float32
    )
    normed_two_part = normed_two_part + lax.dot_general(
        up_grad, up_back, contract_last, preferred_element_type=jnp.float32
    )
    gate_weight_grad = lax.dot_general(
        normed_two, gate_grad, contract_rows, preferred_element_type=jnp.float32
    )
    up_weight_grad = lax.dot_general(
        normed_two, up_grad, contract_rows, preferred_element_type=jnp.float32
    )
    feed_grads = (
        lax.psum_scatter(gate_weight_grad, ("fsdp", "ctx"), scatter_dimension=0, tiled=True),
        lax.psum_scatter(up_weight_grad, ("fsdp", "ctx"), scatter_dimension=0, tiled=True),
        lax.psum_scatter(down_weight_grad, ("fsdp", "ctx"), scatter_dimension=0, tiled=True),
    )
    normed_two_grad = lax.psum_scatter(
        normed_two_part.reshape(seq_count, block_len, model_width).astype(jnp.bfloat16),
        "tp",
        scatter_dimension=1,
        tiled=True,
    ).astype(jnp.float32)
    gain_two_grad = jnp.sum(normed_two_grad * unit_two, (0, 1))
    scaled_two = normed_two_grad * gain_two
    middle_grad = upstream_half + scale_two * (
        scaled_two - unit_two * jnp.mean(scaled_two * unit_two, -1, keepdims=True)
    )
    branch_half = middle_grad.astype(jnp.bfloat16)
    branch_low = lax.all_gather(branch_half, "tp", axis=1, tiled=True).reshape(
        row_count, model_width
    )
    mixed_grad = jnp.dot(branch_low, out_back, preferred_element_type=jnp.float32).astype(
        jnp.bfloat16
    )
    out_weight_grad = lax.dot_general(
        branch_low, mixed, contract_rows, preferred_element_type=jnp.float32
    )
    mixed_heads = mixed_grad.reshape(seq_count, block_len, kv_local, GROUP, HD)

    def attend_back(pieces):
        query_one, pack_one, own_segment, all_segments, log_one, grad_one = pieces
        key_one = pack_one[..., :HD]
        value_one = pack_one[..., HD:]
        masked = masked_scores(query_one, key_one, own_segment, all_segments, first_row)
        probability = jnp.exp(masked - log_one)
        value_grad = jnp.einsum(
            "hgqk,qhgd->khd",
            probability.astype(jnp.bfloat16),
            grad_one,
            preferred_element_type=jnp.float32,
        )
        prob_grad = jnp.einsum(
            "qhgd,khd->hgqk", grad_one, value_one, preferred_element_type=jnp.float32
        )
        centre = jnp.sum(probability * prob_grad, -1, keepdims=True)
        score_grad = (probability * (prob_grad - centre)).astype(jnp.bfloat16)
        query_grad = jnp.einsum(
            "hgqk,khd->qhgd", score_grad, key_one, preferred_element_type=jnp.float32
        ) * HD ** (-0.5)
        key_grad = jnp.einsum(
            "hgqk,qhgd->khd", score_grad, query_one, preferred_element_type=jnp.float32
        ) * HD ** (-0.5)
        return (query_grad, jnp.concatenate([key_grad, value_grad], -1))

    query_grads, pack_grads = lax.map(
        attend_back, (queries, kv_all, own_segments, segments, log_totals, mixed_heads)
    )
    pack_sum = lax.psum_scatter(
        pack_grads.astype(jnp.bfloat16), "ctx", scatter_dimension=1, tiled=True
    ).astype(jnp.float32)
    query_turned = rotate(query_grads, cosine[:, :, None, None], -sine_table[:, :, None, None])
    key_turned = rotate(pack_sum[..., :HD], cosine[:, :, None], -sine_table[:, :, None])
    grouped_grad = jnp.concatenate(
        [query_turned, key_turned[:, :, :, None], pack_sum[:, :, :, None, HD:]], 3
    )
    projected_grad = grouped_grad.reshape(row_count, kv_local * per_group).astype(jnp.bfloat16)
    bias_grad = jnp.sum(projected_grad.astype(jnp.float32), 0).reshape(kv_local, per_group)
    normed_one_part = lax.dot_general(
        projected_grad, qkv_back, contract_last, preferred_element_type=jnp.float32
    )
    qkv_weight_grad = lax.dot_general(
        normed, projected_grad, contract_rows, preferred_element_type=jnp.float32
    )
    qkv_shaped = qkv_weight_grad.reshape(model_width, kv_local, per_group)
    attention_grads = (
        lax.psum_scatter(qkv_shaped, ("fsdp", "ctx"), scatter_dimension=0, tiled=True),
        lax.psum_scatter(out_weight_grad, ("fsdp", "ctx"), scatter_dimension=0, tiled=True),
    )
    normed_one_grad = lax.psum_scatter(
        normed_one_part.reshape(seq_count, block_len, model_width).astype(jnp.bfloat16),
        "tp",
        scatter_dimension=1,
        tiled=True,
    ).astype(jnp.float32)
    unit_one_half = own_rows(unit_one.reshape(seq_count, block_len, model_width))
    scale_one_half = own_rows(scale_one.reshape(seq_count, block_len, 1))
    gain_one_grad = jnp.sum(normed_one_grad * unit_one_half, (0, 1))
    scaled_one = normed_one_grad * gain_one
    input_half = middle_grad + scale_one_half * (
        scaled_one - unit_one_half * jnp.mean(scaled_one * unit_one_half, -1, keepdims=True)
    )
    gain_pair = jnp.stack([gain_one_grad, gain_two_grad])[None]
    gathered = (
        lax.all_gather(input_half.astype(jnp.bfloat16), "tp", axis=1, tiled=True).astype(
            input_half.dtype
        ),
        lax.all_gather(gain_pair.astype(jnp.bfloat16), "tp", axis=0, tiled=True).astype(
            gain_pair.dtype
        ),
    )
    input_grad = gathered[0]
    gain_total = jnp.sum(gathered[1], 0)
    small_grads = lax.psum((gain_total, bias_grad), ("fsdp", "ctx"))
    return (
        block_out,
        input_grad,
        small_grads[0][0],
        attention_grads[0],
        small_grads[1],
        attention_grads[1],
        small_grads[0][1],
        feed_grads[0],
        feed_grads[1],
        feed_grads[2],
    )


def solution(mesh):
    return jax.shard_map(
        shards,
        mesh=mesh,
        in_specs=(
            P("fsdp", "ctx", None),
            P("fsdp", "ctx", None),
            P("fsdp", None),
            P("fsdp", "ctx"),
            P(),
            P(("fsdp", "ctx"), "tp", None),
            P("tp", None),
            P(("fsdp", "ctx"), "tp"),
            P(),
            P(("fsdp", "ctx"), "tp"),
            P(("fsdp", "ctx"), "tp"),
            P(("fsdp", "ctx"), "tp"),
        ),
        out_specs=(
            P("fsdp", ("ctx", "tp"), None),
            P("fsdp", "ctx", None),
            P(),
            P(("fsdp", "ctx"), "tp", None),
            P("tp", None),
            P(("fsdp", "ctx"), "tp"),
            P(),
            P(("fsdp", "ctx"), "tp"),
            P(("fsdp", "ctx"), "tp"),
            P(("fsdp", "ctx"), "tp"),
        ),
        check_vma=False,
    )
```

profile of v0, /device:TPU:0, one launch (start us, length us, event | category | flops | bytes accessed | tf_op | source)
XLA Modules:
  0.0 1616.5 jit_solution(670635166496155173)
XLA Ops:
  10.7 54.7 %all_gather.35 = bf16[896,1,576]{2,0,1:T(8,128)(2,1)S(1)} all-gather(bf16[56,1,576]{2,0,1:T(8,128)(2,1)} %param.21), channel_id=1, replica_groups=mesh['fsdp'=4,'ctx'=4,'tp'=2] {'fsdp','ctx'}, dimensions={0}, use_global_device_ids=true | all-gather | bytes 1096704 | tf_op jit(solution)/shard_map/all_gather | solution.py:69
  84.3 54.6 %all_gather.37 = bf16[896,448]{1,0:T(8,128)(2,1)} all-gather(bf16[56,448]{1,0:T(8,128)(2,1)S(1)} %copy-done.37), channel_id=1, replica_groups=mesh['fsdp'=4,'ctx'=4,'tp'=2] {'fsdp','ctx'}, dimensions={0}, use_global_device_ids=true | all-gather | bytes 852992 | tf_op jit(solution)/shard_map/all_gather | solution.py:70
  138.9 81.7 %while.26 = (s32[]{:T(128)}, bf16[2,512,1,7,64]{1,4,3,2,0:T(8,128)(2,1)}, f32[2,1,7,512,1]{3,2,4,1,0:T(8,128)S(1)}, bf16[2,2048,1,128]{1,3,2,0:T(8,128)(2,1)}, s...) while((s32[]{:T(128)}, ...), condition=%wide.region_4.5_spmd.clone, body=%wide.region_1.4_spmd.sunk.clone | while | flops 1970271232 | bytes 102723752 | solution.py:108
  141.0 11.9 fusion.158
  152.9 12.8 fusion.159
  165.8 13.0 fusion.160
  181.8 11.9 fusion.158
  193.8 12.8 fusion.159
  206.7 13.0 fusion.160
  220.6 4.1 convolution_convert_fusion.2
  226.9 4.7 reduce-scatter.16.cloned.1.call-done
  237.0 9.5 all-gather.10.cloned.1.call-done
  246.5 81.2 %all-gather.14.cloned.1.call-done = bf16[896,2432]{1,0:T(8,128)(2,1)} async-done(((bf16[56,2432]{1,0:T(8,128)(2,1)}), bf16[896,2432]{1,0:T(8,128)(2,1)}) %all-gather.14.cloned.1.call-update) | async-done | bytes 4358160 | tf_op jit(solution)/shard_map/all_gather | solution.py:122
  327.8 10.4 fusion.84
  338.2 68.3 %all-gather.12.cloned.1.call-done = bf16[896,2432]{1,0:T(8,128)(2,1)} async-done(((bf16[56,2432]{1,0:T(8,128)(2,1)}), bf16[896,2432]{1,0:T(8,128)(2,1)}) %all-gather.12.cloned.1.call-update) | async-done | bytes 4358160 | tf_op jit(solution)/shard_map/all_gather | solution.py:121
  406.5 10.5 fusion.83
  416.9 68.2 %all-gather.16.cloned.1.call-done = bf16[896,2432]{1,0:T(8,128)(2,1)} async-done(((bf16[56,2432]{1,0:T(8,128)(2,1)}), bf16[896,2432]{1,0:T(8,128)(2,1)}) %all-gather.16.cloned.1.call-update) | async-done | bytes 4358160 | tf_op jit(solution)/shard_map/all_gather | solution.py:123
  485.1 17.8 %multiply_convert_fusion = (bf16[1024,2432]{1,0:T(8,128)(2,1)}, bf16[1024,2432]{1,0:T(8,128)(2,1)}, bf16[1024,2432]{1,0:T(8,128)(2,1)}) fusion(f32[1024,2432]{1,0:T(8,128)} %fusion.83, f32[1024,2432]{1,0:T(8,128)} %fusion.84, bf16[1024,896]{1,0:T(8,128)(2,1)} %bitcast.347, bf16[896,2432]{1,0:T(8,128)(2,1)} %all-gather.16.cloned.1.call-done), kind=kOutput, calls=%fused_computation.67 | convolution fusion | flops 4500094976 | bytes 41058304 | tf_op jit(solution)/shard_map/dot_general | solution.py:161
  502.9 7.6 fusion.85
  510.5 8.9 add_convert_fusion
  519.5 8.1 reduce-scatter.20.cloned.1.call-done
  531.9 11.4 all-gather.18.cloned.1.call-done
  549.1 188.6 %while.27 = (s32[]{:T(128)}, f32[2,512,1,7,64]{1,4,3,2,0:T(8,128)}, bf16[2,2048,1,128]{1,3,2,0:T(8,128)(2,1)}, bf16[2,2048,1,128]{1,3,2,0:T(8,128)(2,1)}, s32[2,...) while((s32[]{:T(128)}, f32[2,512,1,7,64]{1,4,3,2,0:T(8,128)}, ...), condition=%wide.region_12.13_spmd.clone, body=%wide.region_10.12_spmd.sunk.clone | while | flops 4768363520 | bytes 251635968 | solution.py:235
  551.7 11.8 fusion.167
  563.5 21.3 %fusion.169 = (f32[7,512]{1,0:T(8,128)S(1)}, f32[1,7,512,2048]{2,3,1,0:T(8,128)}) fusion(f32[2048,512,7]{1,0,2:T(8,128)} %fusion.167, f32[7,512]{1,0:T(8,128)S(1)} %dynamic-slice_bitcast_fusion.11, bf16[2,512,1,7,64]{1,4,3,2,0:T(8,128)(2,1)S(1)} %get-tuple-element.480, s32[]{:T(128)S(6)} %copy.121, ...), kind=kOutput, calls=%fused_computation.29.clone.1.clone | convolution fusion | flops 976220672 | bytes 60520452 | tf_op jit(solution)/shard_map/while/body/eval_jaxpr/qhgd,khd->hgqk/dot_general | solution.py:31
  584.8 25.0 %fusion.170 = bf16[7,512,2048]{1,2,0:T(8,128)(2,1)} fusion(f32[1,7,512,2048]{2,3,1,0:T(8,128)} %get-tuple-element.416, f32[2048,512,7]{1,0,2:T(8,128)} %fusion.167, f32[7,512]{1,0:T(8,128)S(1)} %get-tuple-element.417), kind=kLoop, calls=%fused_computation.32.clone.1.clone | loop fusion | flops 22020096 | bytes 73414656 | tf_op jit(solution)/shard_map/reshape.37
  609.7 13.9 fusion.172
  623.6 9.8 fusion.173
  633.5 7.9 fusion.171
  645.7 11.8 fusion.167
  657.5 21.3 %fusion.169 = (f32[7,512]{1,0:T(8,128)S(1)}, f32[1,7,512,2048]{2,3,1,0:T(8,128)}) fusion(f32[2048,512,7]{1,0,2:T(8,128)} %fusion.167, f32[7,512]{1,0:T(8,128)S(1)} %dynamic-slice_bitcast_fusion.11, bf16[2,512,1,7,64]{1,4,3,2,0:T(8,128)(2,1)S(1)} %get-tuple-element.480, s32[]{:T(128)S(6)} %copy.121, ...), kind=kOutput, calls=%fused_computation.29.clone.1.clone | convolution fusion | flops 976220672 | bytes 60520452 | tf_op jit(solution)/shard_map/while/body/eval_jaxpr/qhgd,khd->hgqk/dot_general | solution.py:31
  678.8 25.0 %fusion.170 = bf16[7,512,2048]{1,2,0:T(8,128)(2,1)} fusion(f32[1,7,512,2048]{2,3,1,0:T(8,128)} %get-tuple-element.416, f32[2048,512,7]{1,0,2:T(8,128)} %fusion.167, f32[7,512]{1,0:T(8,128)S(1)} %get-tuple-element.417), kind=kLoop, calls=%fused_computation.32.clone.1.clone | loop fusion | flops 22020096 | bytes 73414656 | tf_op jit(solution)/shard_map/reshape.37
  703.8 13.9 fusion.172
  717.7 9.8 fusion.173
  727.5 7.9 fusion.171
  740.5 25.8 %reduce-scatter.22.cloned.1.call-done = bf16[2,512,1,128]{1,3,2,0:T(8,128)(2,1)} async-done(((bf16[2,2048,1,128]{1,3,2,0:T(8,128)(2,1)}), bf16[2,512,1,128]{1,3,2,0:T(8,128)(2,1)}) %reduce-scatter.22.cloned.1.call-update) | async-done | bytes 262160 | tf_op jit(solution)/shard_map/reduce_scatter | solution.py:238
  773.6 9.6 convolution_convert_fusion.1
  786.0 8.6 reduce-scatter.18.cloned.1.call-done
  794.6 3.8 fusion.56
  798.4 11.9 convolution_bitcast_fusion.1
  813.2 3.7 copy.77
  822.3 11.4 fusion.88
  833.8 10.7 fusion.87
  848.3 48.3 %all-reduce.4 = (f32[2,896]{1,0:T(2,128)S(1)}, f32[1,576]{1,0:T(1,128)}) all-reduce(f32[2,896]{1,0:T(2,128)S(1)} %convert_reduce_fusion.1, f32[1,576]{1,0:T(1,128)S(1)} %reshape.576), channel_id=1, replica_groups=mesh['fsdp'=4,'ctx'=4,'tp'=2] {'fsdp','ctx'}, use_global_device_ids=true, to_apply=%region_19.20 | all-reduce | flops 2368 | bytes 18944 | tf_op jit(solution)/shard_map/psum | solution.py:283
  900.8 243.7 %all-reduce.8.cloned.1.call-done = (f32[896,1,576]{2,1,0:T(1,128)}, f32[896,2432]{0,1:T(8,128)}) async-done(((f32[896,1,576]{2,1,0:T(1,128)}, f32[896,2432]{0,1:T(8,128)}), (f32[896,1,576]{2,1,0:T(1,128)}, f32[896,2432]{0,1:T(8,128)})) %all-reduce.8.cloned.1.call-update) | async-done | bytes 10780688
  1149.4 80.0 %reduce-scatter.26.cloned.1.call-done = f32[56,448]{1,0:T(8,128)} async-done(((f32[896,448]{1,0:T(8,128)}), f32[56,448]{1,0:T(8,128)}) %reduce-scatter.26.cloned.1.call-update) | async-done | bytes 100368 | tf_op jit(solution)/shard_map/reduce_scatter | solution.py:257
  1229.4 189.6 %reduce-scatter.30.cloned.1.call-done = f32[56,2432]{1,0:T(8,128)} async-done(((f32[896,2432]{1,0:T(8,128)}), f32[56,2432]{1,0:T(8,128)}) %reduce-scatter.30.cloned.1.call-update) | async-done | bytes 544784
  1419.0 190.7 %reduce-scatter.28.cloned.1.call-done = f32[56,2432]{1,0:T(8,128)} async-done(((f32[896,2432]{1,0:T(8,128)}), f32[56,2432]{1,0:T(8,128)}) %reduce-scatter.28.cloned.1.call-update) | async-done | bytes 544784
  (248 shorter events, 87.3 us)
Async XLA Ops:
  7.2 58.2 %copy-start.3 = (bf16[2,512,896]{2,1,0:T(8,128)(2,1)S(1)}, bf16[2,512,896]{2,1,0:T(8,128)(2,1)}, u32[]{:S(2)}) copy-start(bf16[2,512,896]{2,1,0:T(8,128)(2,1)} %param.16) | copy-start | bytes 5505028
  7.2 131.7 %all-gather.8.cloned.1.call-start = ((), (), s32[]{:S(2)}) async-start(), calls=%async_computation.8 | async-start | bytes 1310720 | tf_op jit(solution)/shard_map/all_gather | solution.py:93
  8.1 59.7 %copy-start.35 = (f32[896]{0:T(1024)}, f32[896]{0:T(1024)S(1)}, u32[]{:S(2)}) copy-start(f32[896]{0:T(1024)S(1)} %convert_element_type.184) | copy-start | bytes 10756
  10.7 57.0 %copy-start.40 = (f32[2,512]{1,0:T(2,128)}, f32[2,512]{1,0:T(2,128)S(1)}, u32[]{:S(2)}) copy-start(f32[2,512]{1,0:T(2,128)S(1)} %add_rsqrt_fusion) | copy-start | bytes 12292
  71.8 3.5 copy-start.45
  75.2 3.4 copy-start.2
  76.0 5.4 copy-start.21
  76.9 154.7 %reduce-scatter.16.cloned.1.call-start = ((), (), s32[]{:S(2)}) async-start(), calls=%async_computation.9 | async-start | bytes 2752512 | tf_op jit(solution)/shard_map/reduce_scatter | solution.py:113
  83.5 55.4 %copy-start.31 = (f32[2,1,7,512,1]{3,2,4,1,0:T(8,128)S(1)}, f32[2,1,7,512,1]{3,2,4,1,0:T(8,128)}, u32[]{:S(2)}) copy-start(f32[2,1,7,512,1]{3,2,4,1,0:T(8,128)} %custom-call) | copy-start | bytes 86020
  83.5 55.4 %copy-start.32 = (s32[2,512]{1,0:T(2,128)S(1)}, s32[2,512]{1,0:T(2,128)}, u32[]{:S(2)}) copy-start(s32[2,512]{1,0:T(2,128)} %constant_dynamic-slice_fusion.5) | copy-start | bytes 12292
  152.9 12.9 copy-start.13
  193.8 12.9 copy-start.13
  220.6 4.2 copy-start.4
  224.8 21.7 %all-gather.10.cloned.1.call-start = ((), (), s32[]{:S(2)}) async-start(), calls=%async_computation.10 | async-start | bytes 2752512 | tf_op jit(solution)/shard_map/all_gather | solution.py:130
  226.9 303.3 %copy-start.33 = (f32[896]{0:T(1024)}, f32[896]{0:T(1024)S(1)}, u32[]{:S(2)}) copy-start(f32[896]{0:T(1024)S(1)} %convert_element_type.195) | copy-start | bytes 10756
  233.7 296.5 %copy-start = (f32[2,256,896]{2,1,0:T(8,128)}, f32[2,256,896]{2,1,0:T(8,128)S(1)}, u32[]{:S(2)}) copy-start(f32[2,256,896]{2,1,0:T(8,128)S(1)} %get-tuple-element.243) | copy-start | bytes 5505028
  233.7 296.5 %copy-start.38 = (f32[2,256]{1,0:T(2,128)}, f32[2,256]{1,0:T(2,128)S(1)}, u32[]{:S(2)}) copy-start(f32[2,256]{1,0:T(2,128)S(1)} %add_rsqrt_fusion.1) | copy-start | bytes 6148
  235.1 92.7 %all-gather.14.cloned.1.call-start = ((), (), s32[]{:S(2)}) async-start(), calls=%async_computation.12 | async-start | bytes 4630528 | tf_op jit(solution)/shard_map/all_gather | solution.py:122
  235.6 170.8 %all-gather.12.cloned.1.call-start = ((), (), s32[]{:S(2)}) async-start(), calls=%async_computation.11 | async-start | bytes 4630528 | tf_op jit(solution)/shard_map/all_gather | solution.py:121
  236.2 248.9 %all-gather.16.cloned.1.call-start = ((), (), s32[]{:S(2)}) async-start(), calls=%async_computation.13 | async-start | bytes 4630528 | tf_op jit(solution)/shard_map/all_gather | solution.py:123
  236.8 290.8 %reduce-scatter.20.cloned.1.call-start = ((), (), s32[]{:S(2)}) async-start(), calls=%async_computation.15 | async-start | bytes 2752512 | tf_op jit(solution)/shard_map/reduce_scatter | solution.py:187
  485.1 17.8 %copy-start.47 = (bf16[896,2432]{1,0:T(8,128)(2,1)S(1)}, bf16[896,2432]{1,0:T(8,128)(2,1)}, u32[]{:S(2)}) copy-start(bf16[896,2432]{1,0:T(8,128)(2,1)} %all-gather.12.cloned.1.call-done) | copy-start | bytes 13074436
  502.9 7.6 copy-start.51
  519.5 23.8 %all-gather.18.cloned.1.call-start = ((), (), s32[]{:S(2)}) async-start(), calls=%async_computation.16 | async-start | bytes 2752512 | tf_op jit(solution)/shard_map/all_gather | solution.py:199
  531.8 234.5 %reduce-scatter.22.cloned.1.call-start = ((), (), s32[]{:S(2)}) async-start(), calls=%async_computation.17 | async-start | bytes 1310720 | tf_op jit(solution)/shard_map/reduce_scatter | solution.py:238
  623.6 9.8 copy-start.7
  633.5 7.9 copy-start.28
  717.7 9.8 copy-start.7
  727.5 7.9 copy-start.28
  737.8 45.6 %reduce-scatter.24.cloned.1.call-start = ((), (), s32[]{:S(2)}) async-start(), calls=%async_computation.18 | async-start | bytes 2752512 | tf_op jit(solution)/shard_map/reduce_scatter | solution.py:259
  739.9 28.3 %copy-start.22 = (f32[2,512,32]{1,2,0:T(8,128)S(1)}, f32[2,512,32]{1,2,0:T(8,128)}, u32[]{:S(2)}) copy-start(f32[2,512,32]{1,2,0:T(8,128)} %copy-done.21) | copy-start | bytes 393220
  739.9 28.3 %copy-start.24 = (f32[2,512,1,32]{1,3,0,2:T(8,128)S(1)}, f32[2,512,1,32]{1,3,0,2:T(8,128)}, u32[]{:S(2)}) copy-start(f32[2,512,1,32]{1,3,0,2:T(8,128)} %copy-done.23) | copy-start | bytes 393220
  740.5 30.0 %copy-start.26 = (bf16[896,1,576]{2,0,1:T(8,128)(2,1)S(1)}, bf16[896,1,576]{2,0,1:T(8,128)(2,1)}, u32[]{:S(2)}) copy-start(bf16[896,1,576]{2,0,1:T(8,128)(2,1)} %copy-done.25) | copy-start | bytes 3096580
  773.6 21.0 %reduce-scatter.18.cloned.1.call-start = ((), (), s32[]{:S(2)}) async-start(), calls=%async_computation.14 | async-start | bytes 2752512 | tf_op jit(solution)/shard_map/reduce_scatter | solution.py:140
  773.6 9.8 copy-start.41
  773.6 9.8 copy-start.36
  783.3 11.3 copy-start.1
  783.3 11.3 copy-start.6
  783.3 11.3 copy-start.34
  783.3 11.3 copy-start.39
  783.3 11.2 copy-start.43
  783.4 113.9 %all-gather.20.cloned.1.call-start = ((), (), s32[]{:S(2)}) async-start(), calls=%async_computation.19 | async-start | bytes 2752512 | tf_op jit(solution)/shard_map/all_gather | solution.py:274
  798.4 11.9 copy-start.11
  798.4 346.2 %all-reduce.8.cloned.1.call-start = ((), (), s32[]{:S(2)}) async-start(), calls=%async_computation.23 | async-start | bytes 22020096
  816.9 412.5 %reduce-scatter.26.cloned.1.call-start = ((), (), s32[]{:S(2)}) async-start(), calls=%async_computation.20 | async-start | bytes 1949696 | tf_op jit(solution)/shard_map/reduce_scatter | solution.py:257
  819.6 2.7 copy-start.48
  822.0 597.0 %reduce-scatter.30.cloned.1.call-start = ((), (), s32[]{:S(2)}) async-start(), calls=%async_computation.22 | async-start | bytes 9261056
  833.7 776.0 %reduce-scatter.28.cloned.1.call-start = ((), (), s32[]{:S(2)}) async-start(), calls=%async_computation.21 | async-start | bytes 9261056
  (27 other events, 44.5 us)
Sparse Core Ops, SparseCore 0:
  77.0 31.9 all-gather.7
  224.9 6.6 reduce-scatter.15
  235.2 11.3 all-gather.9
  249.4 78.2 all-gather.13
  330.7 75.7 all-gather.11
  409.3 75.7 all-gather.15
  519.6 7.9 reduce-scatter.19
  531.9 11.3 all-gather.17
  738.0 28.3 reduce-scatter.21
  773.7 7.9 reduce-scatter.23
  784.0 10.5 reduce-scatter.17
  798.5 11.3 all-gather.19
  817.4 327.0 all-reduce.7
  1147.3 81.9 reduce-scatter.25
  1232.1 186.8 reduce-scatter.29
  1421.8 187.9 reduce-scatter.27
where the time goes:
time: 1620 us
  waiting for transfers between devices  992 us (61%)
  matrix products  295 us (18%)
  blocking collectives  159 us (10%)
  other arithmetic  113 us (7%)
  local copies, waits for them, and re-layouts  40.6 us (3%)
    unnamed x19, waiting for transfers between devices  626 us
    all_gather x1, waiting for transfers between devices, shards(): lax.all_gather(up_weight, ('fsdp', 'ctx'), axis=0, tiled=True)  81.2 us
    reduce_scatter x1, waiting for transfers between devices, shards(): lax.psum_scatter(out_weight_grad, ('fsdp', 'ctx'), scatter_dimension=0, t...  80 us
    all_gather x1, waiting for transfers between devices, shards(): lax.all_gather(gate_weight, ('fsdp', 'ctx'), axis=0, tiled=True)  68.3 us
    all_gather x1, waiting for transfers between devices, shards(): lax.all_gather(down_weight, ('fsdp', 'ctx'), axis=0, tiled=True)  68.2 us
    dot_general x4, matrix products, masked_scores(): jnp.einsum('qhgd,khd->hgqk', query_one, key_one, preferred_element_type=j...  66.4 us
    all_gather x1, blocking collectives, shards(): lax.all_gather(qkv_weight, ('fsdp', 'ctx'), axis=0, tiled=True)  54.7 us
    all_gather x1, blocking collectives, shards(): lax.all_gather(out_weight, ('fsdp', 'ctx'), axis=0, tiled=True)  54.6 us
  transfers between devices with their start and end apart: 16, of which 13 were waited for; matrix products, arithmetic and copies ran while one was open for 6% of the time, Pallas kernels for 0%

commit v1 on v0

--- a/solution.py
+++ b/solution.py
@@ -10,6 +10,24 @@
 masked_value = -1e30
 contract_rows = (((0,), (0,)), ((), ()))
 contract_last = (((1,), (1,)), ((), ()))
+
+
+def collect(value, axis, dim):
+    ways, here, hop = (lax.axis_size(axis), lax.axis_index(axis), value.shape[dim])
+    shape = [n * ways if d == dim else n for d, n in enumerate(value.shape)]
+    full = lax.dynamic_update_slice_in_dim(
+        jnp.zeros(shape, value.dtype), value, here * hop, axis=dim
+    )
+    going_up = going_down = value
+    for far in range(1, ways // 2 + 1):
+        going_up = lax.ppermute(going_up, axis, [(d, (d + 1) % ways) for d in range(ways)])
+        full = lax.dynamic_update_slice_in_dim(full, going_up, (here - far) % ways * hop, axis=dim)
+        if 2 * far < ways:
+            going_down = lax.ppermute(going_down, axis, [(d, (d - 1) % ways) for d in range(ways)])
+            full = lax.dynamic_update_slice_in_dim(
+                full, going_down, (here + far) % ways * hop, axis=dim
+            )
+    return full
 
 
 def rotary_tables(positions):
@@ -67,7 +85,7 @@
 
     attention_full = (
         lax.all_gather(qkv_weight, ("fsdp", "ctx"), axis=0, tiled=True),
-        lax.all_gather(out_weight, ("fsdp", "ctx"), axis=0, tiled=True),
+        collect(out_weight, ("fsdp", "ctx"), 0),
     )
     qkv_full = attention_full[0].reshape(model_width, kv_local * per_group)
     out_full = attention_full[1]

time: 1620 us -> 1670 us (1.031)
  starting transfers between devices: 1.04 us -> 42.9 us
    ppermute x0 -> x15, starting transfers between devices: none -> 42.1 us  [the longest x7 41.8 us: collect(): lax.ppermute(going_down, axis, [(d, (d - 1) % ways) for d in range(ways)])]
  transfers between devices with their start and end apart: 16 -> 31, of which waited for: 13 -> 24; matrix products, arithmetic and copies ran while one was open for 6% -> 7% of each run, Pallas kernels for 0% -> 0%
where the time goes in v1:
time: 1670 us
  waiting for transfers between devices  993 us (59%)
  matrix products  295 us (18%)
  blocking collectives  155 us (9%)
  other arithmetic  112 us (7%)
  local copies, waits for them, and re-layouts  50.1 us (3%)
  starting transfers between devices  42.9 us (3%)
    unnamed x19, waiting for transfers between devices  626 us
    all_gather x1, waiting for transfers between devices, shards(): lax.all_gather(gate_weight, ('fsdp', 'ctx'), axis=0, tiled=True)  81.2 us
    reduce_scatter x1, waiting for transfers between devices, shards(): lax.psum_scatter(out_weight_grad, ('fsdp', 'ctx'), scatter_dimension=0, t...  79.3 us
    all_gather x1, waiting for transfers between devices, shards(): lax.all_gather(down_weight, ('fsdp', 'ctx'), axis=0, tiled=True)  68.3 us
    all_gather x1, waiting for transfers between devices, shards(): lax.all_gather(up_weight, ('fsdp', 'ctx'), axis=0, tiled=True)  68 us
    dot_general x4, matrix products, masked_scores(): jnp.einsum('qhgd,khd->hgqk', query_one, key_one, preferred_element_type=j...  66.5 us
    all_gather x1, blocking collectives, shards(): lax.all_gather(qkv_weight, ('fsdp', 'ctx'), axis=0, tiled=True)  54.7 us
    another operation x4, other arithmetic  50.5 us
  transfers between devices with their start and end apart: 31, of which 24 were waited for; matrix products, arithmetic and copies ran while one was open for 7% of the time, Pallas kernels for 0%

profile of v1, /device:TPU:0, one launch (start us, length us, event | category | flops | bytes accessed | tf_op | source)
XLA Modules:
  0.0 1665.5 jit_solution(12029237201135259335)
XLA Ops:
  10.0 54.7 %all_gather.34 = bf16[896,1,576]{2,0,1:T(8,128)(2,1)S(1)} all-gather(bf16[56,1,576]{2,0,1:T(8,128)(2,1)} %param.21), channel_id=1, replica_groups=mesh['fsdp'=4,'ctx'=4,'tp'=2] {'fsdp','ctx'}, dimensions={0}, use_global_device_ids=true | all-gather | bytes 1096704 | tf_op jit(solution)/shard_map/all_gather | solution.py:87
  85.8 6.1 collective-permute-start.3
  94.9 6.1 collective-permute-start.5
  103.9 6.1 collective-permute-start.7
  111.8 6.1 collective-permute-start.9
  153.8 79.8 %while.26 = (s32[]{:T(128)}, bf16[2,512,1,7,64]{1,4,3,2,0:T(8,128)(2,1)S(1)}, f32[2,1,7,512,1]{3,2,4,1,0:T(8,128)S(1)}, bf16[2,2048,1,128]{1,3,2,0:T(8,128)(2,1)...) while((s32[]{:T(128)}, ...), condition=%wide.region_4.5_spmd.clone, body=%wide.region_1.4_spmd.sunk.clone | while | flops 1970271232 | bytes 95383656 | solution.py:126
  155.9 11.9 fusion.158
  167.8 12.8 fusion.159
  180.6 13.0 fusion.160
  195.8 11.9 fusion.158
  207.7 12.8 fusion.159
  220.5 13.0 fusion.160
  240.8 8.7 reduce-scatter.16.cloned.1.call-done
  254.8 9.7 all-gather.10.cloned.1.call-done
  264.5 81.2 %all-gather.12.cloned.1.call-done = bf16[896,2432]{1,0:T(8,128)(2,1)} async-done(((bf16[56,2432]{1,0:T(8,128)(2,1)}), bf16[896,2432]{1,0:T(8,128)(2,1)}) %all-gather.12.cloned.1.call-update) | async-done | bytes 4358160 | tf_op jit(solution)/shard_map/all_gather | solution.py:139
  345.7 10.6 fusion.83
  356.4 68.0 %all-gather.14.cloned.1.call-done = bf16[896,2432]{1,0:T(8,128)(2,1)} async-done(((bf16[56,2432]{1,0:T(8,128)(2,1)}), bf16[896,2432]{1,0:T(8,128)(2,1)}) %all-gather.14.cloned.1.call-update) | async-done | bytes 4358160 | tf_op jit(solution)/shard_map/all_gather | solution.py:140
  424.4 10.4 fusion.84
  434.8 68.3 %all-gather.16.cloned.1.call-done = bf16[896,2432]{1,0:T(8,128)(2,1)} async-done(((bf16[56,2432]{1,0:T(8,128)(2,1)}), bf16[896,2432]{1,0:T(8,128)(2,1)}) %all-gather.16.cloned.1.call-update) | async-done | bytes 4358160 | tf_op jit(solution)/shard_map/all_gather | solution.py:141
  503.1 16.9 %multiply_convert_fusion = (bf16[1024,2432]{1,0:T(8,128)(2,1)}, bf16[1024,2432]{1,0:T(8,128)(2,1)S(1)}, bf16[1024,2432]{1,0:T(8,128)(2,1)}) fusion(f32[1024,2432]{1,0:T(8,128)} %fusion.83, f32[1024,2432]{1,0:T(8,128)} %fusion.84, bf16[1024,896]{1,0:T(8,128)(2,1)} %bitcast.347, bf16[896,2432]{1,0:T(8,128)(2,1)} %all-gather.16.cloned.1.call-done), kind=kOutput, calls=%fused_computation.67 | convolution fusion | flops 4500094976 | bytes 41058304 | tf_op jit(solution)/shard_map/dot_general | solution.py:179
  520.0 9.6 fusion.85
  529.6 6.7 add_convert_fusion
  536.4 8.1 reduce-scatter.20.cloned.1.call-done
  548.8 50.4 %all_gather.41 = bf16[896,448]{1,0:T(8,128)(2,1)S(1)} all-gather(bf16[56,448]{1,0:T(8,128)(2,1)S(1)} %copy-done.27), channel_id=1, replica_groups=mesh['fsdp'=4,'ctx'=4,'tp'=2] {'fsdp','ctx'}, dimensions={0}, use_global_device_ids=true | all-gather | bytes 852992 | tf_op jit(solution)/shard_map/all_gather | solution.py:167
  604.7 187.2 %while.27 = (s32[]{:T(128)}, f32[2,512,1,7,64]{1,4,3,2,0:T(8,128)}, bf16[2,2048,1,128]{1,3,2,0:T(8,128)(2,1)}, bf16[2,2048,1,128]{1,3,2,0:T(8,128)(2,1)}, s32[2,...) while((s32[]{:T(128)}, f32[2,512,1,7,64]{1,4,3,2,0:T(8,128)}, ...), condition=%wide.region_12.13_spmd.clone, body=%wide.region_10.12_spmd.sunk.clone | while | flops 4768363520 | bytes 228568192 | solution.py:253
  606.2 11.8 fusion.167
  619.0 21.3 %fusion.169 = (f32[7,512]{1,0:T(8,128)S(1)}, f32[1,7,512,2048]{2,3,1,0:T(8,128)}) fusion(f32[2048,512,7]{1,0,2:T(8,128)} %fusion.167, f32[7,512]{1,0:T(8,128)S(1)} %dynamic-slice_bitcast_fusion.11, bf16[2,512,1,7,64]{1,4,3,2,0:T(8,128)(2,1)S(1)} %get-tuple-element.480, s32[]{:T(128)} %get-tuple-element.463, ...), kind=kOutput, calls=%fused_computation.29.clone.1.clone | convolution fusion | flops 976220672 | bytes 60520452 | tf_op jit(solution)/shard_map/while/body/eval_jaxpr/qhgd,khd->hgqk/dot_general | solution.py:49
  640.3 25.0 %fusion.170 = bf16[7,512,2048]{1,2,0:T(8,128)(2,1)} fusion(f32[1,7,512,2048]{2,3,1,0:T(8,128)} %get-tuple-element.416, f32[2048,512,7]{1,0,2:T(8,128)} %fusion.167, f32[7,512]{1,0:T(8,128)S(1)} %get-tuple-element.417), kind=kLoop, calls=%fused_computation.32.clone.1.clone | loop fusion | flops 22020096 | bytes 73414656 | tf_op jit(solution)/shard_map/reshape.37
  665.3 9.7 fusion.173
  675.0 13.9 fusion.172
  689.7 8.8 fusion.171
  699.5 11.8 fusion.167
  712.3 21.3 %fusion.169 = (f32[7,512]{1,0:T(8,128)S(1)}, f32[1,7,512,2048]{2,3,1,0:T(8,128)}) fusion(f32[2048,512,7]{1,0,2:T(8,128)} %fusion.167, f32[7,512]{1,0:T(8,128)S(1)} %dynamic-slice_bitcast_fusion.11, bf16[2,512,1,7,64]{1,4,3,2,0:T(8,128)(2,1)S(1)} %get-tuple-element.480, s32[]{:T(128)} %get-tuple-element.463, ...), kind=kOutput, calls=%fused_computation.29.clone.1.clone | convolution fusion | flops 976220672 | bytes 60520452 | tf_op jit(solution)/shard_map/while/body/eval_jaxpr/qhgd,khd->hgqk/dot_general | solution.py:49
  733.6 25.0 %fusion.170 = bf16[7,512,2048]{1,2,0:T(8,128)(2,1)} fusion(f32[1,7,512,2048]{2,3,1,0:T(8,128)} %get-tuple-element.416, f32[2048,512,7]{1,0,2:T(8,128)} %fusion.167, f32[7,512]{1,0:T(8,128)S(1)} %get-tuple-element.417), kind=kLoop, calls=%fused_computation.32.clone.1.clone | loop fusion | flops 22020096 | bytes 73414656 | tf_op jit(solution)/shard_map/reshape.37
  758.6 9.7 fusion.173
  768.3 13.9 fusion.172
  783.1 8.7 fusion.171
  794.6 20.9 %reduce-scatter.22.cloned.1.call-done = bf16[2,512,1,128]{1,3,2,0:T(8,128)(2,1)} async-done(((bf16[2,2048,1,128]{1,3,2,0:T(8,128)(2,1)}), bf16[2,512,1,128]{1,3,2,0:T(8,128)(2,1)}) %reduce-scatter.22.cloned.1.call-update) | async-done | bytes 262160 | tf_op jit(solution)/shard_map/reduce_scatter | solution.py:256
  822.9 9.6 convolution_convert_fusion.1
  835.2 8.6 reduce-scatter.18.cloned.1.call-done
  847.6 11.9 convolution_bitcast_fusion.1
  871.6 11.5 fusion.88
  883.1 10.8 fusion.87
  897.7 48.3 %all-reduce.4 = (f32[2,896]{1,0:T(2,128)S(1)}, f32[1,576]{1,0:T(1,128)}) all-reduce(f32[2,896]{1,0:T(2,128)S(1)} %convert_reduce_fusion.1, f32[1,576]{1,0:T(1,128)S(1)} %reshape.576), channel_id=1, replica_groups=mesh['fsdp'=4,'ctx'=4,'tp'=2] {'fsdp','ctx'}, use_global_device_ids=true, to_apply=%region_19.20 | all-reduce | flops 2368 | bytes 18944 | tf_op jit(solution)/shard_map/psum | solution.py:301
  950.2 243.6 %all-reduce.8.cloned.1.call-done = (f32[896,1,576]{2,1,0:T(1,128)}, f32[896,2432]{0,1:T(8,128)}) async-done(((f32[896,1,576]{2,1,0:T(1,128)}, f32[896,2432]{0,1:T(8,128)}), (f32[896,1,576]{2,1,0:T(1,128)}, f32[896,2432]{0,1:T(8,128)})) %all-reduce.8.cloned.1.call-update) | async-done | bytes 10780688
  1198.6 79.3 %reduce-scatter.26.cloned.1.call-done = f32[56,448]{1,0:T(8,128)} async-done(((f32[896,448]{1,0:T(8,128)}), f32[56,448]{1,0:T(8,128)}) %reduce-scatter.26.cloned.1.call-update) | async-done | bytes 100368 | tf_op jit(solution)/shard_map/reduce_scatter | solution.py:275
  1277.9 190.1 %reduce-scatter.30.cloned.1.call-done = f32[56,2432]{1,0:T(8,128)} async-done(((f32[896,2432]{1,0:T(8,128)}), f32[56,2432]{1,0:T(8,128)}) %reduce-scatter.30.cloned.1.call-update) | async-done | bytes 544784
  1468.0 190.7 %reduce-scatter.28.cloned.1.call-done = f32[56,2432]{1,0:T(8,128)} async-done(((f32[896,2432]{1,0:T(8,128)}), f32[56,2432]{1,0:T(8,128)}) %reduce-scatter.28.cloned.1.call-update) | async-done | bytes 544784
  (299 shorter events, 139.4 us)
Async XLA Ops:
  7.2 57.6 %copy-start.3 = (bf16[2,512,896]{2,1,0:T(8,128)(2,1)S(1)}, bf16[2,512,896]{2,1,0:T(8,128)(2,1)}, u32[]{:S(2)}) copy-start(bf16[2,512,896]{2,1,0:T(8,128)(2,1)} %param.16) | copy-start | bytes 5505028
  7.2 57.5 %copy-start.44 = (bf16[1,576]{1,0:T(2,128)(2,1)S(1)}, bf16[1,576]{1,0:T(2,128)(2,1)}, u32[]{:S(2)}) copy-start(bf16[1,576]{1,0:T(2,128)(2,1)} %param.22) | copy-start | bytes 3460
  7.2 145.7 %all-gather.8.cloned.1.call-start = ((), (), s32[]{:S(2)}) async-start(), calls=%async_computation.8 | async-start | bytes 1310720 | tf_op jit(solution)/shard_map/all_gather | solution.py:111
  8.1 59.0 %copy-start.30 = (f32[896]{0:T(1024)}, f32[896]{0:T(1024)S(1)}, u32[]{:S(2)}) copy-start(f32[896]{0:T(1024)S(1)} %convert_element_type.184) | copy-start | bytes 10756
  10.0 57.1 %copy-start.38 = (f32[2,512]{1,0:T(2,128)}, f32[2,512]{1,0:T(2,128)S(1)}, u32[]{:S(2)}) copy-start(f32[2,512]{1,0:T(2,128)S(1)} %add_rsqrt_fusion) | copy-start | bytes 12292
  74.5 36.7 %copy-start.2 = (f32[2,512,1,9,64]{1,0,4,3,2:T(2,128)}, f32[2,512,1,9,64]{1,0,4,3,2:T(2,128)S(1)}, u32[]{:S(2)}) copy-start(f32[2,512,1,9,64]{1,0,4,3,2:T(2,128)S(1)} %reshape.570) | copy-start | bytes 7077892
  75.3 35.8 %copy-start.17 = (f32[2,512,32]{1,2,0:T(8,128)}, f32[2,512,32]{1,2,0:T(8,128)S(1)}, u32[]{:S(2)}) copy-start(f32[2,512,32]{1,2,0:T(8,128)S(1)} %get-tuple-element.263) | copy-start | bytes 393220
  76.7 172.8 %reduce-scatter.16.cloned.1.call-start = ((), (), s32[]{:S(2)}) async-start(), calls=%async_computation.9 | async-start | bytes 2752512 | tf_op jit(solution)/shard_map/reduce_scatter | solution.py:131
  76.8 7.9 collective-permute-start
  76.9 9.0 collective-permute-start.1
  84.7 9.0 collective-permute-start.2
  85.8 9.0 collective-permute-start.3
  93.6 9.0 collective-permute-start.4
  94.9 9.0 collective-permute-start.5
  102.6 8.6 collective-permute-start.6
  103.9 7.9 collective-permute-start.7
  111.2 8.0 collective-permute-start.8
  111.8 8.1 collective-permute-start.9
  119.2 8.1 collective-permute-start.10
  119.2 16.0 copy-start.25
  119.8 15.9 copy-start.32
  119.8 7.7 collective-permute-start.11
  127.3 7.8 collective-permute-start.12
  127.5 21.4 %collective-permute-start.13 = (bf16[56,448]{1,0:T(8,128)(2,1)S(1)}, bf16[56,448]{1,0:T(8,128)(2,1)}, u32[]{:S(2)}, u32[]{:S(2)}) collective-permute-start(bf16[56,448]{1,0:T(8,128)(2,1)S(1)} %collective-permute-done.11), channel_id=1, source_target_pairs={{0,30},{2,0},{4,2},{6,4},{8,6},{10,8},{12,10},{14,12},{16,14},{18,... | collective-permute-start | bytes 150536 | tf_op jit(solution)/shard_map/ppermute | solution.py:26
  135.0 16.1 collective-permute-start.14
  238.7 25.8 %all-gather.10.cloned.1.call-start = ((), (), s32[]{:S(2)}) async-start(), calls=%async_computation.10 | async-start | bytes 2752512 | tf_op jit(solution)/shard_map/all_gather | solution.py:148
  240.8 306.3 %copy-start.28 = (f32[896]{0:T(1024)}, f32[896]{0:T(1024)S(1)}, u32[]{:S(2)}) copy-start(f32[896]{0:T(1024)S(1)} %convert_element_type.195) | copy-start | bytes 10756
  251.6 295.5 %copy-start = (f32[2,256,896]{2,1,0:T(8,128)}, f32[2,256,896]{2,1,0:T(8,128)S(1)}, u32[]{:S(2)}) copy-start(f32[2,256,896]{2,1,0:T(8,128)S(1)} %get-tuple-element.243) | copy-start | bytes 5505028
  251.7 295.4 %copy-start.36 = (f32[2,256]{1,0:T(2,128)}, f32[2,256]{1,0:T(2,128)S(1)}, u32[]{:S(2)}) copy-start(f32[2,256]{1,0:T(2,128)S(1)} %add_rsqrt_fusion.1) | copy-start | bytes 6148
  253.0 92.7 %all-gather.12.cloned.1.call-start = ((), (), s32[]{:S(2)}) async-start(), calls=%async_computation.11 | async-start | bytes 4630528 | tf_op jit(solution)/shard_map/all_gather | solution.py:139
  253.6 170.8 %all-gather.14.cloned.1.call-start = ((), (), s32[]{:S(2)}) async-start(), calls=%async_computation.12 | async-start | bytes 4630528 | tf_op jit(solution)/shard_map/all_gather | solution.py:140
  254.2 248.9 %all-gather.16.cloned.1.call-start = ((), (), s32[]{:S(2)}) async-start(), calls=%async_computation.13 | async-start | bytes 4630528 | tf_op jit(solution)/shard_map/all_gather | solution.py:141
  254.8 289.7 %reduce-scatter.20.cloned.1.call-start = ((), (), s32[]{:S(2)}) async-start(), calls=%async_computation.15 | async-start | bytes 2752512 | tf_op jit(solution)/shard_map/reduce_scatter | solution.py:205
  536.3 62.8 %all-gather.18.cloned.1.call-start = ((), (), s32[]{:S(2)}) async-start(), calls=%async_computation.16 | async-start | bytes 2752512 | tf_op jit(solution)/shard_map/all_gather | solution.py:217
  548.7 266.9 %reduce-scatter.22.cloned.1.call-start = ((), (), s32[]{:S(2)}) async-start(), calls=%async_computation.17 | async-start | bytes 1310720 | tf_op jit(solution)/shard_map/reduce_scatter | solution.py:256
  792.0 40.7 %reduce-scatter.24.cloned.1.call-start = ((), (), s32[]{:S(2)}) async-start(), calls=%async_computation.18 | async-start | bytes 2752512 | tf_op jit(solution)/shard_map/reduce_scatter | solution.py:277
  794.1 23.4 %copy-start.18 = (f32[2,512,32]{1,2,0:T(8,128)S(1)}, f32[2,512,32]{1,2,0:T(8,128)}, u32[]{:S(2)}) copy-start(f32[2,512,32]{1,2,0:T(8,128)} %copy-done.17) | copy-start | bytes 393220
  794.1 23.4 %copy-start.20 = (f32[2,512,1,32]{1,3,0,2:T(8,128)S(1)}, f32[2,512,1,32]{1,3,0,2:T(8,128)}, u32[]{:S(2)}) copy-start(f32[2,512,1,32]{1,3,0,2:T(8,128)} %copy-done.19) | copy-start | bytes 393220
  794.6 25.1 %copy-start.22 = (bf16[896,1,576]{2,0,1:T(8,128)(2,1)S(1)}, bf16[896,1,576]{2,0,1:T(8,128)(2,1)}, u32[]{:S(2)}) copy-start(bf16[896,1,576]{2,0,1:T(8,128)(2,1)} %copy-done.21) | copy-start | bytes 3096580
  822.8 21.0 %reduce-scatter.18.cloned.1.call-start = ((), (), s32[]{:S(2)}) async-start(), calls=%async_computation.14 | async-start | bytes 2752512 | tf_op jit(solution)/shard_map/reduce_scatter | solution.py:158
  832.5 11.3 copy-start.6
  832.5 11.3 copy-start.29
  832.6 114.1 %all-gather.20.cloned.1.call-start = ((), (), s32[]{:S(2)}) async-start(), calls=%async_computation.19 | async-start | bytes 2752512 | tf_op jit(solution)/shard_map/all_gather | solution.py:292
  847.6 12.0 copy-start.9
  847.6 346.2 %all-reduce.8.cloned.1.call-start = ((), (), s32[]{:S(2)}) async-start(), calls=%async_computation.23 | async-start | bytes 22020096
  866.2 411.8 %reduce-scatter.26.cloned.1.call-start = ((), (), s32[]{:S(2)}) async-start(), calls=%async_computation.20 | async-start | bytes 1949696 | tf_op jit(solution)/shard_map/reduce_scatter | solution.py:275
  871.3 596.8 %reduce-scatter.30.cloned.1.call-start = ((), (), s32[]{:S(2)}) async-start(), calls=%async_computation.22 | async-start | bytes 9261056
  883.1 775.7 %reduce-scatter.28.cloned.1.call-start = ((), (), s32[]{:S(2)}) async-start(), calls=%async_computation.21 | async-start | bytes 9261056
  (36 other events, 168.7 us)
Sparse Core Ops, SparseCore 0:
  76.9 31.2 all-gather.7
  238.8 10.6 reduce-scatter.15
  253.1 11.3 all-gather.9
  267.4 78.2 all-gather.11
  348.6 75.7 all-gather.13
  427.3 75.7 all-gather.15
  536.4 7.9 reduce-scatter.19
  548.8 11.3 all-gather.17
  792.1 23.3 reduce-scatter.21
  822.9 8.0 reduce-scatter.23
  833.2 10.4 reduce-scatter.17
  847.7 11.3 all-gather.19
  866.6 327.0 all-reduce.7
  1196.6 81.2 reduce-scatter.25
  1280.7 187.3 reduce-scatter.29
  1470.8 187.9 reduce-scatter.27
